TPU v7x, 512 devices: a whole 4x8x8 slice. The times are simulated.
512 devices in a mesh: replica: 8 (over y_lo, core), shard: 64 (over z, y_hi, x).
Axes of the slice: x: 4, y: 8 (y_hi: 2, y_lo: 4; y = y_hi * 4 + y_lo), z: 8, core: 2. Of those that a mesh axis runs over, the one named last changes fastest.
Arguments:
- gradients: bfloat16 [8, 2, 64, 1024, 256], P('replica', None, None, 'shard'), may hold values from -36 to 36
- momentum: float32 [8, 64, 1024, 256], P('replica', None, 'shard'), may hold values from -3 to 3
- params: float32 [64, 1024, 256], P(None, ('shard', 'replica')), may hold values from -6 to 6
- outer_moment: float32 [64, 1024, 256], P(None, ('shard', 'replica')), may hold values from -2 to 2
- shadow: float32 [64, 1024, 256], P(None, ('shard', 'replica')), may hold values from -6 to 6
Outputs:
- new_params: float32 [64, 1024, 256], P(None, ('shard', 'replica'))
- new_outer_moment: float32 [64, 1024, 256], P(None, ('shard', 'replica'))
- new_shadow: float32 [64, 1024, 256], P(None, ('shard', 'replica'))
- new_momentum: float32 [8, 64, 1024, 256], P('replica', None, 'shard')
All inputs are finite; a program needn't handle non-finite values.
Results may differ from a plain program's by a relative error of at most 0.0085.
Values may be sent and summed in bfloat16 or wider, within the bound.
A program may use at most 64 MiB of HBM per device.

v0:
```python
import math

import jax
import jax.numpy as jnp
from jax import lax
from jax.sharding import PartitionSpec as P

D = 1024
INNER = 2
NS_ITERS = 5


quintic_a = 3.4445
quintic_b = -4.775
quintic_c = 2.0315
inner_beta = 0.95
outer_mu = 0.9
outer_rate = 0.7
shadow_decay = 0.9


def split_up(shard, dim, size):
    before, after = (shard.shape[:dim], shard.shape[dim + 1 :])
    return jnp.moveaxis(shard.reshape(*before, size, -1, *after), dim, 0)


def sum_at_owner(shard, axis, dim):
    size = lax.axis_size(axis)
    tiles = lax.all_to_all(split_up(shard, dim, size), axis, 0, 0, tiled=True)
    return jnp.sum(tiles.astype(jnp.float32), axis=0)


def newton_schulz(blocks):
    squares = jnp.sum(jnp.square(blocks.astype(jnp.float32)), axis=(1, 2), keepdims=True)
    current = (blocks.astype(jnp.float32) / (jnp.sqrt(squares) + 1e-07)).astype(jnp.bfloat16)
    for repeat in range(NS_ITERS):
        gram_block = jnp.einsum(
            "mdi,mdj->mij", current, current, preferred_element_type=jnp.float32
        ).astype(jnp.bfloat16)
        square = jnp.einsum(
            "mij,mjk->mik", gram_block, gram_block, preferred_element_type=jnp.float32
        )
        polynomial = (quintic_b * gram_block.astype(jnp.float32) + quintic_c * square).astype(
            jnp.bfloat16
        )
        product = jnp.einsum(
            "mdi,mij->mdj", current, polynomial, preferred_element_type=jnp.float32
        )
        current = (quintic_a * current.astype(jnp.float32) + product).astype(jnp.bfloat16)
    return current


def body(gradients, momentum, params, outer_moment, shadow):
    scale_step = 0.2 * math.sqrt(D)
    shard_count = lax.axis_size("shard")
    replica_count = lax.axis_size("replica")
    moment_now = momentum[0]
    updates = []
    for position in range(INNER):
        grad_now = gradients[0, position].astype(jnp.float32)
        moment_now = inner_beta * moment_now + grad_now
        updates.append((grad_now + inner_beta * moment_now).astype(jnp.bfloat16))
    owned_total = None
    stacked = jnp.stack(updates)
    owned = lax.all_to_all(stacked, "shard", split_axis=1, concat_axis=2, tiled=True)
    orthos = newton_schulz(owned.reshape((-1,) + owned.shape[2:])).reshape(owned.shape)
    owned_total = scale_step * orthos[0].astype(jnp.float32)
    position = 1
    owned_total = owned_total + scale_step * orthos[position].astype(jnp.float32)
    mat_count = owned_total.shape[0]
    rows_each = owned_total.shape[1] // (shard_count * replica_count)
    width = owned_total.shape[2]
    grouped = owned_total.reshape((mat_count, shard_count, replica_count, rows_each, width))
    reduced = sum_at_owner(grouped.astype(jnp.bfloat16), "replica", 2)
    reduced = reduced.reshape((mat_count, shard_count, rows_each, width))
    placed = lax.all_to_all(
        reduced.astype(jnp.bfloat16), "shard", split_axis=1, concat_axis=0, tiled=True
    ).astype(reduced.dtype)
    summed = placed.reshape((mat_count * shard_count, rows_each, width))
    outer_delta = summed / replica_count
    new_outer = outer_mu * outer_moment + outer_delta
    new_params = params - outer_rate * (outer_delta + outer_mu * new_outer)
    new_shadow = shadow_decay * shadow + (1.0 - shadow_decay) * new_params
    return (new_params, new_outer, new_shadow, moment_now[None])


def solution(mesh):
    in_specs = (
        P("replica", None, None, "shard", None),
        P("replica", None, "shard", None),
        P(None, ("shard", "replica"), None),
        P(None, ("shard", "replica"), None),
        P(None, ("shard", "replica"), None),
    )
    out_specs = (
        P(None, ("shard", "replica"), None),
        P(None, ("shard", "replica"), None),
        P(None, ("shard", "replica"), None),
        P("replica", None, "shard", None),
    )
    return jax.shard_map(body, mesh=mesh, in_specs=in_specs, out_specs=out_specs, check_vma=False)
```

profile of v0, /device:TPU:1, one launch (start us, length us, event | category | flops | bytes accessed | tf_op | source)
XLA Modules:
  0.0 101.9 jit_solution(3864957524999742524)
XLA Ops:
  0.6 2.9 %fusion.14 = (f32[1,64,16,256]{3,2,1,0:T(8,128)}, bf16[1,64,16,256]{3,2,0,1:T(8,128)(2,1)S(1)}, bf16[1,64,16,256]{3,2,0,1:T(8,128)(2,1)S(1)}) fusion(f32[1,64,16,256]{3,2,1,0:T(8,128)} %param.6, bf16[1,2,64,16,256]{4,3,2,1,0:T(8,128)(2,1)} %param.5), kind=kLoop, calls=%fused_computation.38 | loop fusion | flops 2883584 | bytes 4194304
  3.5 0.1 pad_maximum_fusion
  3.6 45.4 %all_to_all.23 = bf16[2,64,16,256]{3,2,0,1:T(8,128)(2,1)S(1)} all-to-all(bf16[2,64,16,256]{3,2,0,1:T(8,128)(2,1)S(1)} %pad_maximum_fusion), channel_id=1, replica_groups=mesh['replica'=8,'shard'=64] {'shard'}, dimensions={1} | all-to-all | bytes 2097152 | tf_op jit(solution)/shard_map/all_to_all | solution.py:65
  49.0 0.4 multiply_reduce_fusion
  49.4 0.3 copy.15
  49.7 0.2 fusion
  49.9 0.5 convolution_convert_fusion.4
  50.5 0.6 add_convert_fusion.4
  51.1 0.5 convolution_convert_fusion.3
  51.6 0.6 add_convert_fusion.3
  52.3 0.5 convolution_convert_fusion.2
  52.8 0.6 add_convert_fusion.2
  53.4 0.5 convolution_convert_fusion.1
  54.0 0.6 add_convert_fusion.1
  54.6 0.5 convolution_convert_fusion
  55.1 0.6 add_convert_fusion
  55.8 0.2 multiply_convert_fusion
  56.0 0.0 copy-start.2
  56.0 0.2 convert_element_type.209
  56.2 0.4 copy.29
  56.6 25.9 %all_to_all.24 = bf16[8,1,64,1,2,256]{5,4,2,3,1,0:T(2,128)(2,1)S(1)} all-to-all(bf16[8,1,64,1,2,256]{5,4,2,3,1,0:T(2,128)(2,1)S(1)} %bitcast.65), channel_id=1, replica_groups=mesh['replica'=8,'shard'=64] {'replica'}, dimensions={0} | all-to-all | bytes 1048576 | tf_op jit(solution)/shard_map/all_to_all | solution.py:29
  82.5 0.5 reduce_sum.22
  83.0 17.8 %all_to_all.25 = bf16[1,64,2,256]{3,2,0,1:T(2,128)(2,1)S(1)} all-to-all(bf16[1,64,2,256]{3,2,0,1:T(2,128)(2,1)S(1)} %bitcast.66), channel_id=1, replica_groups=mesh['replica'=8,'shard'=64] {'shard'}, dimensions={1} | all-to-all | bytes 131072 | tf_op jit(solution)/shard_map/all_to_all | solution.py:76
  100.9 1.0 multiply_add_fusion
  (6 shorter events, 0.0 us)
Async XLA Ops:
  55.9 44.9 %copy-start = (f32[64,2,256]{2,1,0:T(2,128)S(1)}, f32[64,2,256]{2,1,0:T(2,128)}, u32[]{:S(2)}) copy-start(f32[64,2,256]{2,1,0:T(2,128)} %param.9) | copy-start | bytes 393220
  56.0 44.9 %copy-start.1 = (f32[64,2,256]{2,1,0:T(2,128)S(1)}, f32[64,2,256]{2,1,0:T(2,128)}, u32[]{:S(2)}) copy-start(f32[64,2,256]{2,1,0:T(2,128)} %param.7) | copy-start | bytes 393220
  56.0 44.9 %copy-start.2 = (f32[64,2,256]{2,1,0:T(2,128)S(1)}, f32[64,2,256]{2,1,0:T(2,128)}, u32[]{:S(2)}) copy-start(f32[64,2,256]{2,1,0:T(2,128)} %param.8) | copy-start | bytes 393220
where the time goes:
time: 102 us
  blocking collectives  89.2 us (87%)
  matrix products  5.79 us (6%)
  other arithmetic  5.3 us (5%)
    all_to_all x1, blocking collectives, body(): lax.all_to_all(stacked, 'shard', split_axis=1, concat_axis=2, tiled=True)  45.4 us
    all_to_all x1, blocking collectives, sum_at_owner(): tiles = lax.all_to_all(split_up(shard, dim, size), axis, 0, 0, tiled=True)  25.9 us
    all_to_all x1, blocking collectives, body(): lax.all_to_all(reduced.astype(jnp.bfloat16), 'shard', split_axis=1, conca...  17.8 us
    dot_general x5, matrix products, newton_schulz(): jnp.einsum('mdi,mij->mdj', current, polynomial, preferred_element_type=jn...  3.18 us
    unnamed x1, other arithmetic  2.85 us
    dot_general x5, matrix products, newton_schulz(): jnp.einsum('mdi,mdj->mij', current, current, preferred_element_type=jnp.f...  2.61 us

commit v1 on v0

v1 whole, which is shorter than its diff:
```python
import functools
import math

import jax
import jax.numpy as jnp
from jax import lax
from jax.experimental import pallas as pl
from jax.experimental.pallas import tpu as pltpu
from jax.sharding import PartitionSpec as P

D = 1024
FF = 256
INNER = 2
NS_ITERS = 5
MATS = 64
ROWS = 16

quintic_a = 3.4445
quintic_b = -4.775
quintic_c = 2.0315
inner_beta = 0.95
outer_mu = 0.9
outer_rate = 0.7
shadow_decay = 0.9
scale_step = 0.2 * math.sqrt(D)

MESH = pl.DeviceIdType.MESH
f32, bf16 = jnp.float32, jnp.bfloat16
NT = (((1,), (1,)), ((), ()))
NN = (((1,), (0,)), ((), ()))


def place():
    replica, shard = lax.axis_index("replica"), lax.axis_index("shard")
    core, y_lo = replica % 2, replica // 2
    x, y_hi, z = shard % 4, (shard // 4) % 2, shard // 8
    return x, y_hi * 4 + y_lo, z, core


def device(x, y, z, core):
    return {"replica": (y % 4) * 2 + core, "shard": z * 8 + (y // 4) * 4 + x}


def spread(j):
    j = (3 * j) % 8
    half = (j + 1) // 2
    return (8 + half * (2 * (j % 2) - 1)) % 8


def offsets(i):
    outer, inner = i // 8, i % 8
    return spread((5 * inner + outer) % 8), spread(inner)


def dot(a, b, dims):
    return lax.dot_general(a, b, dims, preferred_element_type=f32)


def newton_schulz(update):
    wide = update.astype(f32)
    squares = jnp.sum(wide * wide)
    current = (wide / (jnp.sqrt(squares) + 1e-07)).astype(bf16).T
    for _ in range(NS_ITERS):
        gram = dot(current, current, NT).astype(bf16)
        square = dot(gram, gram, NN)
        poly = (quintic_b * gram.astype(f32) + quintic_c * square).astype(bf16)
        current = (quintic_a * current.astype(f32) + dot(poly, current, NN)).astype(bf16)
    return current


def wait_bytes(ref, sem):
    pltpu.make_async_copy(ref, ref, sem).wait()


def exchange_kernel(u0, u1, out, own, first, delta, parts, reduced, gathered,
                    send_a, recv_a, send_b, recv_b, send_c, recv_c):
    x, y, z, core = place()
    mine = z * 8 + y
    shard = z * 8 + (y // 4) * 4 + x
    x_of = lambda y_m: (y % 4 + y_m) % 4
    self_a = x_of(y) == x
    self_c = core == z // 4

    barrier = pltpu.get_barrier_semaphore()

    def greet(x, y, z, core):
        pl.semaphore_signal(barrier, 1, device_id=device(x, y, z, core), device_id_type=MESH)

    def greet_a(i, _):
        sx, syh, sz = i % 4, (i // 4) % 2, i // 8
        sy = syh * 4 + (x + 8 - y) % 4

        @pl.when(jnp.logical_not((sx == x) & (sy == y) & (sz == z)))
        def _():
            greet(sx, sy, sz, core)

        return 0

    def greet_c(i, _):
        sy, sz, sc = i % 8, i // 8, z // 4

        @pl.when(jnp.logical_not((sy == y) & (sz == z) & (sc == core)))
        def _():
            greet(x, sy, sz, sc)

        return 0

    lax.fori_loop(0, 64, greet_a, 0)
    for j in range(1, 8):
        greet((x + j // 2) % 4, y, z, (core + j) % 2)
    lax.fori_loop(0, 64, greet_c, 0)
    pl.semaphore_wait(
        barrier, 64 + 7 + 64 - self_a.astype(jnp.int32) - self_c.astype(jnp.int32)
    )

    my_rows = pl.ds(pl.multiple_of(shard * ROWS, ROWS), ROWS)
    for k, u in enumerate((u0, u1)):

        def send(i, _):
            dy, dz = offsets(i)
            y_m, z_m = (y + dy) % 8, (z + dz) % 8
            x_m = x_of(y_m)
            m = z_m * 8 + y_m
            here = (dy == 0) & (dz == 0) & self_a

            @pl.when(jnp.logical_not(here))
            def _():
                pltpu.make_async_remote_copy(
                    u.at[m], own.at[k, my_rows], send_a.at[k], recv_a.at[k],
                    device_id=device(x_m, y_m, z_m, core), device_id_type=MESH,
                ).start()

            @pl.when(here)
            def _():
                pltpu.make_async_copy(u.at[m], own.at[k, my_rows], recv_a.at[k]).start()

            return 0

        lax.fori_loop(0, 64, send, 0)

    wait_bytes(own.at[0], recv_a.at[0])
    first[...] = newton_schulz(own[0])
    wait_bytes(own.at[1], recv_a.at[1])
    second = newton_schulz(own[1])
    total = (scale_step * first[...].astype(f32) + scale_step * second.astype(f32)).astype(bf16).T
    for zz in range(8):
        for yh in range(2):
            for xx in range(4):
                row = zz * 128 + yh * 64 + xx * 16
                delta[xx * 2 + zz // 4, pl.ds((zz % 4) * 32 + yh * 16, 16), :] = total[row : row + 16]

    me = x * 2 + core
    copies = []
    for j in range(1, 8):
        tx, tc = (x + j // 2) % 4, (core + j) % 2
        copy = pltpu.make_async_remote_copy(
            delta.at[tx * 2 + tc], parts.at[j], send_b.at[j], recv_b.at[j],
            device_id=device(tx, y, z, tc), device_id_type=MESH,
        )
        copy.start()
        copies.append(copy)
    summed = delta[me].astype(f32)
    for j, copy in enumerate(copies):
        copy.wait_recv()
        summed = summed + parts[j + 1].astype(f32)
    summed = summed.astype(bf16)
    for i in range(64):
        reduced[i] = summed[2 * i : 2 * i + 2]

    def scatter(i, _):
        yy, tz, tc = i % 8, (i // 8) % 4, i // 32
        ty = (y + yy) % 8
        tz_all = core * 4 + (z + tz) % 4
        tcore = (core + tc) % 2
        piece = (tz_all % 4) * 16 + (ty // 4) * 8 + (ty % 4) * 2 + tcore
        here = (ty == y) & (tz_all == z) & (tcore == core)

        @pl.when(jnp.logical_not(here))
        def _():
            pltpu.make_async_remote_copy(
                reduced.at[piece], gathered.at[mine], send_c, recv_c,
                device_id=device(x, ty, tz_all, tcore), device_id_type=MESH,
            ).start()

        @pl.when(here)
        def _():
            pltpu.make_async_copy(reduced.at[piece], gathered.at[mine], recv_c).start()

        return 0

    lax.fori_loop(0, 64, scatter, 0)
    wait_bytes(gathered, recv_c)
    out[...] = gathered[...]

    for k in range(2):

        @pl.when(self_a)
        def _():
            wait_bytes(own.at[k, pl.ds(0, 63 * ROWS)], send_a.at[k])

        @pl.when(jnp.logical_not(self_a))
        def _():
            wait_bytes(own.at[k], send_a.at[k])

    for copy in copies:
        copy.wait_send()

    @pl.when(self_c)
    def _():
        wait_bytes(reduced.at[pl.ds(0, 63)], send_c)

    @pl.when(jnp.logical_not(self_c))
    def _():
        wait_bytes(reduced, send_c)


def exchange(u0, u1):
    vmem = pl.BlockSpec(memory_space=pltpu.VMEM)
    dma = pltpu.SemaphoreType.DMA
    return pl.pallas_call(
        exchange_kernel,
        out_shape=jax.ShapeDtypeStruct((MATS, 2, FF), bf16),
        in_specs=[vmem, vmem],
        out_specs=vmem,
        scratch_shapes=[
            pltpu.VMEM((INNER, D, FF), bf16),
            pltpu.VMEM((FF, D), bf16),
            pltpu.VMEM((8, 128, FF), bf16),
            pltpu.VMEM((8, 128, FF), bf16),
            pltpu.VMEM((64, 2, FF), bf16),
            pltpu.VMEM((64, 2, FF), bf16),
            dma((INNER,)), dma((INNER,)), dma((8,)), dma((8,)), dma, dma,
        ],
        compiler_params=pltpu.CompilerParams(
            collective_id=0, has_side_effects=True, vmem_limit_bytes=40 << 20
        ),
        name="muon_exchange",
    )(u0, u1)


def body(gradients, momentum, params, outer_moment, shadow):
    replica_count = lax.axis_size("replica")
    moment_now = momentum[0]
    updates = []
    for position in range(INNER):
        grad_now = gradients[0, position].astype(f32)
        moment_now = inner_beta * moment_now + grad_now
        updates.append((grad_now + inner_beta * moment_now).astype(bf16))
    summed = exchange(*updates)
    outer_delta = summed.astype(f32) / replica_count
    new_outer = outer_mu * outer_moment + outer_delta
    new_params = params - outer_rate * (outer_delta + outer_mu * new_outer)
    new_shadow = shadow_decay * shadow + (1.0 - shadow_decay) * new_params
    return (new_params, new_outer, new_shadow, moment_now[None])


def solution(mesh):
    state = P(None, ("shard", "replica"), None)
    momentum = P("replica", None, "shard", None)
    return jax.shard_map(
        body,
        mesh=mesh,
        in_specs=(P("replica", None, None, "shard", None), momentum, state, state, state),
        out_specs=(state, state, state, momentum),
        check_vma=False,
    )
```

time: 102 us -> 74.5 us (0.73)
  blocking collectives: 89.2 us -> 0 us
  Pallas kernels: 0 us -> 69.5 us
  matrix products: 5.79 us -> 0 us
  other arithmetic: 5.3 us -> 4.18 us
    all_to_all x3 -> x0, blocking collectives: 89.2 us -> none  [the longest x1 45.4 us: body(): lax.all_to_all(stacked, 'shard', split_axis=1, concat_axis=2, tiled=True)]
    pallas_call x0 -> x1, Pallas kernels: none -> 69.5 us  [exchange(): pl.pallas_call(exchange_kernel, out_shape=jax.ShapeDtypeStruct((MATS, 2,...]
    dot_general x10 -> x0, matrix products: 5.79 us -> none  [the longest x5 3.18 us: newton_schulz(): jnp.einsum('mdi,mij->mdj', current, polynomial, preferred_element_type=jn...]
    unnamed x1 -> x0, other arithmetic: 2.85 us -> none
    convert_element_type x2 -> x1, other arithmetic: 0.4 us -> 1.97 us  [body(): updates.append((grad_now + inner_beta * moment_now).astype(bf16))]
    add x1, other arithmetic: 0.01 us -> 1.2 us  [body(): moment_now = inner_beta * moment_now + grad_now]
where the time goes in v1:
time: 74.5 us; the launch traced here: 74.4 us
  Pallas kernels  69.5 us (93%)
  other arithmetic  4.18 us (6%)
    pallas_call x1, Pallas kernels, exchange(): pl.pallas_call(exchange_kernel, out_shape=jax.ShapeDtypeStruct((MATS, 2,...  69.5 us
    convert_element_type x1, other arithmetic, body(): updates.append((grad_now + inner_beta * moment_now).astype(bf16))  1.97 us

profile of v1, /device:TPU:1, one launch (start us, length us, event | category | flops | bytes accessed | tf_op | source)
XLA Modules:
  0.0 74.4 jit_solution(67412524524898787)
XLA Ops:
  0.6 0.0 copy-start.2
  0.6 0.0 copy-start.3
  0.7 0.0 copy-start.4
  0.7 0.0 copy-start.1
  0.7 2.0 %fusion.10 = (bf16[64,16,256]{2,1,0:T(8,128)(2,1)S(1)}, bf16[64,16,256]{2,1,0:T(8,128)(2,1)S(1)}) fusion(f32[1,64,16,256]{3,2,1,0:T(8,128)} %param.6, bf16[1,2,64,16,256]{4,3,2,1,0:T(8,128)(2,1)} %param.5), kind=kLoop, calls=%fused_computation.14 | loop fusion | flops 2883584 | bytes 3145728 | tf_op jit(solution)/shard_map/convert_element_type | solution.py:248
  2.6 0.0 copy-start
  2.7 69.5 %muon_exchange.1 = bf16[64,2,256]{2,1,0:T(2,128)(2,1)S(1)} custom-call(bf16[64,16,256]{2,1,0:T(8,128)(2,1)S(1)} %get-tuple-element.8.u0, bf16[64,16,256]{2,1,0:T(8,128)(2,1)S(1)} %get-tuple-element.7.u1), custom_call_target="tpu_custom_call" | custom-call | tf_op jit(solution)/shard_map/muon_exchange/pallas_call | solution.py:220
  72.1 0.0 copy-done.2
  72.1 0.0 copy-done.3
  72.1 0.0 copy-done.4
  72.1 1.0 %multiply_add_fusion = (f32[64,2,256]{2,1,0:T(2,128)}, f32[64,2,256]{2,1,0:T(2,128)}, f32[64,2,256]{2,1,0:T(2,128)}) fusion(f32[64,2,256]{2,1,0:T(2,128)S(1)} %copy-done.2, f32[64,2,256]{2,1,0:T(2,128)S(1)} %copy-done.3, bf16[64,2,256]{2,1,0:T(2,128)(2,1)S(1)} %muon_exchange.1, f32[64,2,256]{2,1,0:T(2,128)S(1)} %copy-done.4), kind=kLoop, calls=%fused_computation.15 | loop fusion | flops 360448 | bytes 851968 | tf_op jit(solution)/shard_map/add | solution.py:253
  73.2 0.0 copy-done.1
  73.2 0.0 copy-done
  73.2 1.2 %fusion.8 = f32[1,64,16,256]{3,2,1,0:T(8,128)} fusion(f32[1,64,16,256]{3,2,1,0:T(8,128)S(1)} %copy-done, bf16[1,2,64,16,256]{4,3,2,1,0:T(8,128)(2,1)S(1)} %copy-done.1), kind=kLoop, calls=%fused_computation.12 | loop fusion | flops 1572864 | bytes 3145728 | tf_op jit(solution)/shard_map/add | solution.py:247
Async XLA Ops:
  0.6 71.5 %copy-start.2 = (f32[64,2,256]{2,1,0:T(2,128)S(1)}, f32[64,2,256]{2,1,0:T(2,128)}, u32[]{:S(2)}) copy-start(f32[64,2,256]{2,1,0:T(2,128)} %param.9) | copy-start | bytes 393220
  0.6 71.5 %copy-start.3 = (f32[64,2,256]{2,1,0:T(2,128)S(1)}, f32[64,2,256]{2,1,0:T(2,128)}, u32[]{:S(2)}) copy-start(f32[64,2,256]{2,1,0:T(2,128)} %param.7) | copy-start | bytes 393220
  0.7 71.5 %copy-start.4 = (f32[64,2,256]{2,1,0:T(2,128)S(1)}, f32[64,2,256]{2,1,0:T(2,128)}, u32[]{:S(2)}) copy-start(f32[64,2,256]{2,1,0:T(2,128)} %param.8) | copy-start | bytes 393220
  0.7 72.5 %copy-start.1 = (bf16[1,2,64,16,256]{4,3,2,1,0:T(8,128)(2,1)S(1)}, bf16[1,2,64,16,256]{4,3,2,1,0:T(8,128)(2,1)}, u32[]{:S(2)}) copy-start(bf16[1,2,64,16,256]{4,3,2,1,0:T(8,128)(2,1)} %param.5) | copy-start | bytes 3145732
  2.6 70.5 %copy-start = (f32[1,64,16,256]{3,2,1,0:T(8,128)S(1)}, f32[1,64,16,256]{3,2,1,0:T(8,128)}, u32[]{:S(2)}) copy-start(f32[1,64,16,256]{3,2,1,0:T(8,128)} %param.6) | copy-start | bytes 3145732

commit v2 on v1

v2 whole, which is shorter than its diff:
```python
import functools
import math

import jax
import jax.numpy as jnp
from jax import lax
from jax.experimental import pallas as pl
from jax.experimental.pallas import tpu as pltpu
from jax.sharding import PartitionSpec as P

D = 1024
FF = 256
INNER = 2
NS_ITERS = 5
MATS = 64
ROWS = 16
CHUNKS = 4
PER_CHUNK = MATS // CHUNKS

quintic_a = 3.4445
quintic_b = -4.775
quintic_c = 2.0315
inner_beta = 0.95
outer_mu = 0.9
outer_rate = 0.7
shadow_decay = 0.9
scale_step = 0.2 * math.sqrt(D)

MESH = pl.DeviceIdType.MESH
f32, bf16 = jnp.float32, jnp.bfloat16
NT = (((1,), (1,)), ((), ()))
NN = (((1,), (0,)), ((), ()))


def place():
    replica, shard = lax.axis_index("replica"), lax.axis_index("shard")
    core, y_lo = rem(replica, 2), div(replica, 2)
    x, y_hi, z = rem(shard, 4), rem(div(shard, 4), 2), div(shard, 8)
    return replica, shard, x, y_hi * 4 + y_lo, z, core


DZ_ORDER = (0, 2, 5, 1, 6, 4, 7, 3)
DY_ORDER = (0, 4, 5, 2, 6, 3, 7, 1)


def rem(a, b):
    return lax.rem(a, jnp.int32(b))


def div(a, b):
    return lax.div(a, jnp.int32(b))


def dot(a, b, dims):
    return lax.dot_general(a, b, dims, preferred_element_type=f32)


def normalized(update):
    wide = update.astype(f32)
    squares = jnp.sum(wide * wide)
    return (wide / (jnp.sqrt(squares) + 1e-07)).astype(bf16)


def polynomial(current):
    gram = dot(current, current, NT).astype(bf16)
    square = dot(gram, gram, NN)
    return (quintic_b * gram.astype(f32) + quintic_c * square).astype(bf16)


def advance(current, poly):
    return (quintic_a * current.astype(f32) + dot(poly, current, NN)).astype(bf16)


def until_last(update):
    current = normalized(update).T
    for _ in range(NS_ITERS - 1):
        current = advance(current, polynomial(current))
    return current, polynomial(current)


def wait_bytes(ref, sem):
    pltpu.make_async_copy(ref, ref, sem).wait()


def exchange_kernel(gradients, momentum, out, new_momentum, grad, moment, updates, own, first, last,
                    delta, swapped, half, parts, reduced, gathered,
                    load, send_a, recv_a, send_s, recv_s, send_b, recv_b, send_c, recv_c):
    replica, shard, x, y, z, core = place()
    mine = z * 8 + y
    y_lo, z_half = rem(y, 4), div(z, 4)
    x_of = lambda y_m: rem(y + y_m, 4)
    self_a = x_of(y) == x
    self_c = core == z_half

    loads = []
    for c in range(CHUNKS):
        part = pl.ds(c * PER_CHUNK, PER_CHUNK)
        loads.append([
            pltpu.make_async_copy(gradients.at[:, part], grad.at[:, part], load.at[c, 0]),
            pltpu.make_async_copy(momentum.at[part], moment.at[part], load.at[c, 1]),
        ])
    for pair in loads:
        for copy in pair:
            copy.start()

    barrier = pltpu.get_barrier_semaphore()

    def greet(replica, shard):
        pl.semaphore_signal(
            barrier, 1, device_id={"replica": replica, "shard": shard}, device_id_type=MESH
        )

    from_replica = rem(x + 8 - y, 4) * 2 + core

    def greet_a(i, _):
        greet(from_replica, rem(shard + i, 64))
        return 0

    lax.fori_loop(1, 64, greet_a, 0, unroll=9)

    @pl.when(jnp.logical_not(self_a))
    def _():
        greet(from_replica, shard)

    other = {"replica": y_lo * 2 + 1 - core, "shard": shard}
    ring = [{"replica": replica, "shard": shard - x + rem(x + j, 4)} for j in range(4)]
    for peer in (other, *ring[1:]):
        greet(**peer)

    for c, pair in enumerate(loads):
        for copy in pair:
            copy.wait()

        def step(i, _):
            m = c * PER_CHUNK + i
            now = moment[m]
            for k in range(INNER):
                wide = grad[k, m].astype(f32)
                now = inner_beta * now + wide
                updates[k, m] = (wide + inner_beta * now).astype(bf16)
            new_momentum[m] = now
            return 0

        lax.fori_loop(0, PER_CHUNK, step, 0, unroll=4)

    pl.semaphore_wait(barrier, 64 + 4 - self_a.astype(jnp.int32))

    my_rows = pl.ds(pl.multiple_of(shard * ROWS, ROWS), ROWS)
    layers = [rem(z + dz, 8) * 8 for dz in DZ_ORDER]
    for k in range(INNER):

        def send(a, _):
            for b in range(8):
                y_m = rem(y + (DY_ORDER[b] + a), 8)
                m = layers[b] + y_m

                def go():
                    pltpu.make_async_remote_copy(
                        updates.at[k, m], own.at[k, my_rows], send_a.at[k], recv_a.at[k],
                        device_id={
                            "replica": rem(y_m, 4) * 2 + core,
                            "shard": layers[b] + div(y_m, 4) * 4 + x_of(y_m),
                        },
                        device_id_type=MESH,
                    ).start()

                if b == 0:
                    pl.when((a > 0) | jnp.logical_not(self_a))(go)
                else:
                    go()
            return 0

        lax.fori_loop(0, 8, send, 0)

        @pl.when(self_a)
        def _():
            pltpu.make_async_copy(updates.at[k, mine], own.at[k, my_rows], recv_a.at[k]).start()

    wait_bytes(own.at[0], recv_a.at[0])
    first[...] = advance(*until_last(own[0]))
    wait_bytes(own.at[1], recv_a.at[1])
    last[...], poly = until_last(own[1])
    swaps = []
    for j in range(4):
        chunk = rem(2 * (1 - core) + j, 4)
        columns = pl.ds(pl.multiple_of(chunk * 256, 256), 256)
        second = advance(last[:, columns], poly)
        total = (scale_step * first[:, columns].astype(f32) + scale_step * second.astype(f32)).astype(bf16).T
        for zz in range(2):
            for yh in range(2):
                for xx in range(4):
                    row = zz * 128 + yh * 64 + xx * 16
                    to = (j % 2) * 64 + zz * 32 + yh * 16
                    delta[j // 2, xx, pl.ds(to, 16), :] = total[row : row + 16]
        if j < 2:
            rows = pl.ds(j * 64, 64)
            copy = pltpu.make_async_remote_copy(
                delta.at[0, :, rows], swapped.at[:, rows], send_s.at[j], recv_s.at[j],
                device_id=other, device_id_type=MESH,
            )
            copy.start()
            swaps.append(copy)

    for copy in swaps:
        copy.wait_recv()
    copies = {}
    for j in (2, 1, 3):
        to = rem(x + j, 4)
        half[j] = (delta[1, to].astype(f32) + swapped[to].astype(f32)).astype(bf16)
        copies[j] = pltpu.make_async_remote_copy(
            half.at[j], parts.at[j], send_b.at[j], recv_b.at[j],
            device_id=ring[j], device_id_type=MESH,
        )
        copies[j].start()
    summed = delta[1, x].astype(f32) + swapped[x].astype(f32)
    for j in (1, 3, 2):
        copies[j].wait_recv()
        summed = summed + parts[j].astype(f32)
    summed = summed.astype(bf16)
    for i in range(64):
        reduced[i] = summed[2 * i : 2 * i + 2]

    def scatter(q, _):
        ty = rem(y + 8 + div(8 - q, 2) * (rem(q, 2) * 2 - 1), 8)
        ty_lo, ty_hi = rem(ty, 4), div(ty, 4)
        for t in (2, 1, 3, 0):
            tz_lo = rem(z + t, 4)
            for tc in range(2):
                tcore = rem(core + tc, 2)
                piece = tz_lo * 16 + ty_hi * 8 + ty_lo * 2 + tcore

                def go():
                    pltpu.make_async_remote_copy(
                        reduced.at[piece], gathered.at[mine], send_c, recv_c,
                        device_id={
                            "replica": ty_lo * 2 + tcore,
                            "shard": core * 32 + tz_lo * 8 + ty_hi * 4 + x,
                        },
                        device_id_type=MESH,
                    ).start()

                if t == 0 and tc == 0:
                    pl.when((q < 7) | jnp.logical_not(self_c))(go)
                else:
                    go()
        return 0

    lax.fori_loop(0, 8, scatter, 0)

    @pl.when(self_c)
    def _():
        piece = rem(z, 4) * 16 + div(y, 4) * 8 + y_lo * 2 + core
        pltpu.make_async_copy(reduced.at[piece], gathered.at[mine], recv_c).start()

    wait_bytes(gathered, recv_c)
    out[...] = gathered[...]

    for k in range(2):

        @pl.when(self_a)
        def _():
            wait_bytes(own.at[k, pl.ds(0, 63 * ROWS)], send_a.at[k])

        @pl.when(jnp.logical_not(self_a))
        def _():
            wait_bytes(own.at[k], send_a.at[k])

    for copy in (*swaps, *copies.values()):
        copy.wait_send()

    @pl.when(self_c)
    def _():
        wait_bytes(reduced.at[pl.ds(0, 63)], send_c)

    @pl.when(jnp.logical_not(self_c))
    def _():
        wait_bytes(reduced, send_c)


def exchange(gradients, momentum):
    vmem = pl.BlockSpec(memory_space=pltpu.VMEM)
    anywhere = pl.BlockSpec(memory_space=pl.ANY)
    dma = pltpu.SemaphoreType.DMA
    return pl.pallas_call(
        exchange_kernel,
        out_shape=(
            jax.ShapeDtypeStruct((MATS, 2, FF), bf16),
            jax.ShapeDtypeStruct((MATS, ROWS, FF), f32),
        ),
        in_specs=[anywhere, anywhere],
        out_specs=(vmem, vmem),
        scratch_shapes=[
            pltpu.VMEM((INNER, MATS, ROWS, FF), bf16),
            pltpu.VMEM((MATS, ROWS, FF), f32),
            pltpu.VMEM((INNER, MATS, ROWS, FF), bf16),
            pltpu.VMEM((INNER, D, FF), bf16),
            pltpu.VMEM((FF, D), bf16),
            pltpu.VMEM((FF, D), bf16),
            pltpu.VMEM((2, 4, 128, FF), bf16),
            pltpu.VMEM((4, 128, FF), bf16),
            pltpu.VMEM((4, 128, FF), bf16),
            pltpu.VMEM((4, 128, FF), bf16),
            pltpu.VMEM((64, 2, FF), bf16),
            pltpu.VMEM((64, 2, FF), bf16),
            dma((CHUNKS, 2)), dma((INNER,)), dma((INNER,)), dma((2,)), dma((2,)), dma((4,)), dma((4,)), dma, dma,
        ],
        compiler_params=pltpu.CompilerParams(
            collective_id=0, has_side_effects=True, vmem_limit_bytes=52 << 20
        ),
        name="muon_exchange",
    )(gradients, momentum)


def outer_kernel(summed, moved, params, outer_moment, shadow, new_params, new_outer, new_shadow,
                 new_momentum, results, done, moved_done):
    keep = pltpu.make_async_copy(moved, new_momentum, moved_done)
    keep.start()
    copies = []
    for c in range(CHUNKS):
        part = pl.ds(c * PER_CHUNK, PER_CHUNK)
        outer_delta = summed[part].astype(f32) / 8
        outer = outer_mu * outer_moment[part] + outer_delta
        weights = params[part] - outer_rate * (outer_delta + outer_mu * outer)
        average = shadow_decay * shadow[part] + (1.0 - shadow_decay) * weights
        for i, (value, to) in enumerate(((weights, new_params), (outer, new_outer), (average, new_shadow))):
            results[i, part] = value
            copy = pltpu.make_async_copy(results.at[i, part], to.at[part], done.at[c, i])
            copy.start()
            copies.append(copy)
    for copy in copies:
        copy.wait()
    keep.wait()


def body(gradients, momentum, params, outer_moment, shadow):
    summed, moved = exchange(gradients[0], momentum[0])
    vmem = pl.BlockSpec(memory_space=pltpu.VMEM)
    anywhere = pl.BlockSpec(memory_space=pl.ANY)
    state = jax.ShapeDtypeStruct((MATS, 2, FF), f32)
    new_params, new_outer, new_shadow, new_momentum = pl.pallas_call(
        outer_kernel,
        out_shape=(state, state, state, jax.ShapeDtypeStruct((MATS, ROWS, FF), f32)),
        in_specs=[vmem] * 5,
        out_specs=(anywhere,) * 4,
        scratch_shapes=[
            pltpu.VMEM((3, MATS, 2, FF), f32),
            pltpu.SemaphoreType.DMA((CHUNKS, 3)),
            pltpu.SemaphoreType.DMA,
        ],
        compiler_params=pltpu.CompilerParams(vmem_limit_bytes=8 << 20),
        name="outer_step",
    )(summed, moved, params, outer_moment, shadow)
    return (new_params, new_outer, new_shadow, new_momentum[None])


def solution(mesh):
    state = P(None, ("shard", "replica"), None)
    momentum = P("replica", None, "shard", None)
    return jax.shard_map(
        body,
        mesh=mesh,
        in_specs=(P("replica", None, None, "shard", None), momentum, state, state, state),
        out_specs=(state, state, state, momentum),
        check_vma=False,
    )
```

time: 74.5 us -> 66.6 us (0.89)
  other arithmetic: 4.18 us -> 0 us
  Pallas kernels: 69.5 us -> 65.8 us
    pallas_call x1 -> x2, Pallas kernels: 69.5 us -> 65.8 us  [the longest x1 64.5 us: exchange(): pl.pallas_call(exchange_kernel, out_shape=(jax.ShapeDtypeStruct((MATS, 2,...]
    add x2 -> x0, other arithmetic: 2.21 us -> none  [the longest x1 1.2 us: body(): moment_now = inner_beta * moment_now + grad_now]
    convert_element_type x1 -> x0, other arithmetic: 1.97 us -> none  [body(): updates.append((grad_now + inner_beta * moment_now).astype(bf16))]
where the time goes in v2:
time: 66.6 us; the launch traced here: 66.5 us
  Pallas kernels  65.8 us (99%)
  between operations  0.69 us (1%)
    pallas_call x1, Pallas kernels, exchange(): pl.pallas_call(exchange_kernel, out_shape=(jax.ShapeDtypeStruct((MATS, 2,...  64.5 us

profile of v2, /device:TPU:1, one launch (start us, length us, event | category | flops | bytes accessed | tf_op | source)
XLA Modules:
  0.0 66.5 jit_solution(1708686128101496171)
XLA Ops:
  0.6 0.0 copy-start
  0.6 0.0 copy-start.1
  0.7 0.0 copy-start.2
  0.7 64.5 %muon_exchange.1 = (bf16[64,2,256]{2,1,0:T(2,128)(2,1)S(1)}, f32[64,16,256]{2,1,0:T(8,128)S(1)}) custom-call(bf16[2,64,16,256]{3,2,1,0:T(8,128)(2,1)} %bitcast.3, f32[64,16,256]{2,1,0:T(8,128)} %bitcast.4), custom_call_target="tpu_custom_call" | custom-call | tf_op jit(solution)/shard_map/muon_exchange/pallas_call | solution.py:284
  65.2 0.0 copy-done
  65.2 0.0 copy-done.1
  65.2 0.0 copy-done.2
  65.2 1.2 %outer_step.1 = (f32[64,2,256]{2,1,0:T(2,128)}, f32[64,2,256]{2,1,0:T(2,128)}, f32[64,2,256]{2,1,0:T(2,128)}, f32[64,16,256]{2,1,0:T(8,128)}) custom-call(bf16[64,2,256]{2,1,0:T(2,128)(2,1)S(1)} %get-tuple-element.10.summed, f32[64,16,256]{2,1,0:T(8,128)S(1)} %get-tuple-element.11.moved, f32[64,2,256]{2,1,0:T(2,128)S(1)} %copy-done, ...), custom_call_target="tpu_custom_call" | custom-call | tf_op jit(solution)/shard_map/outer_step/pallas_call | solution.py:340
Async XLA Ops:
  0.6 64.6 %copy-start = (f32[64,2,256]{2,1,0:T(2,128)S(1)}, f32[64,2,256]{2,1,0:T(2,128)}, u32[]{:S(2)}) copy-start(f32[64,2,256]{2,1,0:T(2,128)} %params.1) | copy-start | bytes 393220
  0.6 64.6 %copy-start.1 = (f32[64,2,256]{2,1,0:T(2,128)S(1)}, f32[64,2,256]{2,1,0:T(2,128)}, u32[]{:S(2)}) copy-start(f32[64,2,256]{2,1,0:T(2,128)} %outer_moment.1) | copy-start | bytes 393220
  0.7 64.6 %copy-start.2 = (f32[64,2,256]{2,1,0:T(2,128)S(1)}, f32[64,2,256]{2,1,0:T(2,128)}, u32[]{:S(2)}) copy-start(f32[64,2,256]{2,1,0:T(2,128)} %shadow.1) | copy-start | bytes 393220

commit v3 on v2

--- a/solution.py
+++ b/solution.py
@@ -41,6 +41,8 @@
 
 DZ_ORDER = (0, 2, 5, 1, 6, 4, 7, 3)
 DY_ORDER = (0, 4, 5, 2, 6, 3, 7, 1)
+ORDER = [((DY_ORDER[b] + a) % 8, DZ_ORDER[b]) for a in range(8) for b in range(8)]
+ORDER.sort(key=lambda o: min(o[0], 8 - o[0]) + min(o[1], 8 - o[1]) <= 2)
 
 
 def rem(a, b):
@@ -55,14 +57,8 @@
     return lax.dot_general(a, b, dims, preferred_element_type=f32)
 
 
-def normalized(update):
-    wide = update.astype(f32)
-    squares = jnp.sum(wide * wide)
-    return (wide / (jnp.sqrt(squares) + 1e-07)).astype(bf16)
-
-
-def polynomial(current):
-    gram = dot(current, current, NT).astype(bf16)
+def polynomial(gram):
+    gram = gram.astype(bf16)
     square = dot(gram, gram, NN)
     return (quintic_b * gram.astype(f32) + quintic_c * square).astype(bf16)
 
@@ -72,10 +68,17 @@
 
 
 def until_last(update):
-    current = normalized(update).T
+    raw = update.T
+    gram = dot(raw, raw, NT)
+    row, column = (lax.broadcasted_iota(jnp.int32, gram.shape, i) for i in range(2))
+    squares = jnp.sum(jnp.where(row == column, gram, 0.0))
+    scale = 1.0 / (jnp.sqrt(squares) + 1e-07)
+    poly = polynomial(gram * scale * scale)
+    current = (raw.astype(f32) * scale).astype(bf16)
     for _ in range(NS_ITERS - 1):
-        current = advance(current, polynomial(current))
-    return current, polynomial(current)
+        current = advance(current, poly)
+        poly = polynomial(dot(current, current, NT))
+    return current, poly
 
 
 def wait_bytes(ref, sem):
@@ -116,7 +119,8 @@
         greet(from_replica, rem(shard + i, 64))
         return 0
 
-    lax.fori_loop(1, 64, greet_a, 0, unroll=9)
+    lax.fori_loop(25, 64, greet_a, 0, unroll=13)
+    lax.fori_loop(1, 25, greet_a, 0, unroll=12)
 
     @pl.when(jnp.logical_not(self_a))
     def _():
@@ -146,35 +150,35 @@
     pl.semaphore_wait(barrier, 64 + 4 - self_a.astype(jnp.int32))
 
     my_rows = pl.ds(pl.multiple_of(shard * ROWS, ROWS), ROWS)
-    layers = [rem(z + dz, 8) * 8 for dz in DZ_ORDER]
-    for k in range(INNER):
-
-        def send(a, _):
-            for b in range(8):
-                y_m = rem(y + (DY_ORDER[b] + a), 8)
-                m = layers[b] + y_m
-
-                def go():
-                    pltpu.make_async_remote_copy(
-                        updates.at[k, m], own.at[k, my_rows], send_a.at[k], recv_a.at[k],
-                        device_id={
-                            "replica": rem(y_m, 4) * 2 + core,
-                            "shard": layers[b] + div(y_m, 4) * 4 + x_of(y_m),
-                        },
-                        device_id_type=MESH,
-                    ).start()
-
-                if b == 0:
-                    pl.when((a > 0) | jnp.logical_not(self_a))(go)
-                else:
-                    go()
-            return 0
-
-        lax.fori_loop(0, 8, send, 0)
+    across = []
+    for dy in range(8):
+        y_m = rem(y + dy, 8)
+        across.append((y_m, rem(y_m, 4) * 2 + core, div(y_m, 4) * 4 + x_of(y_m)))
+    layers = [rem(z + dz, 8) * 8 for dz in range(8)]
+
+    def send(k, _):
+        for dy, dz in ORDER:
+            y_m, to_replica, to_column = across[dy]
+
+            def go():
+                pltpu.make_async_remote_copy(
+                    updates.at[k, layers[dz] + y_m], own.at[k, my_rows], send_a.at[k], recv_a.at[k],
+                    device_id={"replica": to_replica, "shard": layers[dz] + to_column},
+                    device_id_type=MESH,
+                ).start()
+
+            if (dy, dz) == (0, 0):
+                pl.when(jnp.logical_not(self_a))(go)
+            else:
+                go()
 
         @pl.when(self_a)
         def _():
             pltpu.make_async_copy(updates.at[k, mine], own.at[k, my_rows], recv_a.at[k]).start()
+
+        return 0
+
+    lax.fori_loop(0, INNER, send, 0)
 
     wait_bytes(own.at[0], recv_a.at[0])
     first[...] = advance(*until_last(own[0]))

time: 66.6 us -> 65.7 us (0.986)
  Pallas kernels: 65.8 us -> 64.8 us
    pallas_call x1, Pallas kernels: 64.5 us -> 63.6 us  [exchange(): pl.pallas_call(exchange_kernel, out_shape=(jax.ShapeDtypeStruct((MATS, 2,...]
where the time goes in v3:
time: 65.7 us; the launch traced here: 65.5 us
  Pallas kernels  64.8 us (99%)
  between operations  0.69 us (1%)
    pallas_call x1, Pallas kernels, exchange(): pl.pallas_call(exchange_kernel, out_shape=(jax.ShapeDtypeStruct((MATS, 2,...  63.6 us

profile of v3, /device:TPU:1, one launch (start us, length us, event | category | flops | bytes accessed | tf_op | source)
XLA Modules:
  0.0 65.5 jit_solution(841545034940006988)
XLA Ops:
  0.6 0.0 copy-start
  0.6 0.0 copy-start.1
  0.7 0.0 copy-start.2
  0.7 63.6 %muon_exchange.1 = (bf16[64,2,256]{2,1,0:T(2,128)(2,1)S(1)}, f32[64,16,256]{2,1,0:T(8,128)S(1)}) custom-call(bf16[2,64,16,256]{3,2,1,0:T(8,128)(2,1)} %bitcast.3, f32[64,16,256]{2,1,0:T(8,128)} %bitcast.4), custom_call_target="tpu_custom_call" | custom-call | tf_op jit(solution)/shard_map/muon_exchange/pallas_call | solution.py:288
  64.3 0.0 copy-done
  64.3 0.0 copy-done.1
  64.3 0.0 copy-done.2
  64.3 1.2 %outer_step.1 = (f32[64,2,256]{2,1,0:T(2,128)}, f32[64,2,256]{2,1,0:T(2,128)}, f32[64,2,256]{2,1,0:T(2,128)}, f32[64,16,256]{2,1,0:T(8,128)}) custom-call(bf16[64,2,256]{2,1,0:T(2,128)(2,1)S(1)} %get-tuple-element.10.summed, f32[64,16,256]{2,1,0:T(8,128)S(1)} %get-tuple-element.11.moved, f32[64,2,256]{2,1,0:T(2,128)S(1)} %copy-done, ...), custom_call_target="tpu_custom_call" | custom-call | tf_op jit(solution)/shard_map/outer_step/pallas_call | solution.py:344
Async XLA Ops:
  0.6 63.6 %copy-start = (f32[64,2,256]{2,1,0:T(2,128)S(1)}, f32[64,2,256]{2,1,0:T(2,128)}, u32[]{:S(2)}) copy-start(f32[64,2,256]{2,1,0:T(2,128)} %params.1) | copy-start | bytes 393220
  0.6 63.6 %copy-start.1 = (f32[64,2,256]{2,1,0:T(2,128)S(1)}, f32[64,2,256]{2,1,0:T(2,128)}, u32[]{:S(2)}) copy-start(f32[64,2,256]{2,1,0:T(2,128)} %outer_moment.1) | copy-start | bytes 393220
  0.7 63.6 %copy-start.2 = (f32[64,2,256]{2,1,0:T(2,128)S(1)}, f32[64,2,256]{2,1,0:T(2,128)}, u32[]{:S(2)}) copy-start(f32[64,2,256]{2,1,0:T(2,128)} %shadow.1) | copy-start | bytes 393220
